TPU v7x, 32 devices: a whole 2x2x4 slice. The times are simulated.
32 devices in a mesh: dp: 8 (over y, x, core), sp: 4 (over z).
Axes of the slice: x: 2, y: 2, z: 4, core: 2. Of those that a mesh axis runs over, the one named last changes fastest.
Arguments:
- inputs: bfloat16 [16, 2048, 768], P('dp', 'sp'), may hold values from -6 to 6
- out_grad: bfloat16 [16, 2048, 768], P('dp', 'sp'), may hold values from -6 to 6
- segment_ids: int32 [16, 2048], P('dp'), may hold values from 0 to 7, as said below
- positions: int32 [16, 2048], P('dp'), may hold values from 0 to 1023, as said below
- norm1_gain: bfloat16 [768], replicated, may hold values from 0.5 to 1.5
- norm1_bias: bfloat16 [768], replicated, may hold values from -1.75 to 1.75
- norm2_gain: bfloat16 [768], replicated, may hold values from 0.5 to 1.5
- norm2_bias: bfloat16 [768], replicated, may hold values from -1.75 to 1.75
- query_weight: bfloat16 [768, 768], replicated, may hold values from -0.21875 to 0.21875
- query_bias: bfloat16 [768], replicated, may hold values from -1.75 to 1.75
- key_weight: bfloat16 [768, 64], replicated, may hold values from -0.21875 to 0.21875
- key_bias: bfloat16 [16], replicated, may hold values from -1.75 to 1.75
- value_weight: bfloat16 [768, 64], replicated, may hold values from -0.21875 to 0.21875
- value_bias: bfloat16 [64], replicated, may hold values from -1.75 to 1.75
- output_weight: bfloat16 [768, 768], replicated, may hold values from -2.5 to 2.5
- output_bias: bfloat16 [768], replicated, may hold values from -1.75 to 1.75
- hidden_weight: bfloat16 [768, 3072], replicated, may hold values from -0.21875 to 0.21875
- hidden_bias: bfloat16 [3072], replicated, may hold values from -1.75 to 1.75
- down_weight: bfloat16 [3072, 768], replicated, may hold values from -0.109375 to 0.109375
- down_bias: bfloat16 [768], replicated, may hold values from -1.75 to 1.75
Outputs:
- layer_out: bfloat16 [16, 2048, 768], P('dp', 'sp')
- input_grad: float32 [16, 2048, 768], P('dp', 'sp')
- norm1_gain_grad: float32 [768], P('sp')
- norm1_bias_grad: float32 [768], P('sp')
- norm2_gain_grad: float32 [768], P('sp')
- norm2_bias_grad: float32 [768], P('sp')
- query_weight_grad: float32 [768, 768], P('sp')
- query_bias_grad: float32 [768], P('sp')
- key_weight_grad: float32 [768, 64], P('sp')
- key_bias_grad: float32 [16], P('sp')
- value_weight_grad: float32 [768, 64], P('sp')
- value_bias_grad: float32 [64], P('sp')
- output_weight_grad: float32 [768, 768], P('sp')
- output_bias_grad: float32 [768], P('sp')
- hidden_weight_grad: float32 [768, 3072], P('sp')
- hidden_bias_grad: float32 [3072], P('sp')
- down_weight_grad: float32 [3072, 768], P('sp')
- down_bias_grad: float32 [768], P('sp')
Inputs may be any that keep to these rules, and one draw needn't show every extreme that they name: `segment_ids`: document numbers of a row start at 0 and rise by one at each of its 7 boundaries, so every row holds exactly 8 documents; the first document of every row holds exactly 1024 tokens and each other document fewer. `positions`: each token's place counted from 0 at the first token of its document.
All inputs are finite; a program needn't handle non-finite values.
Results may differ from a plain program's by a relative error of at most 0.0085.
The roundings to bfloat16 on the way count: a program that leaves them out, or rounds other values in their place, can miss the bound.
Values may be sent and summed in bfloat16 or wider, within the bound.
No kernel may reach another device: no remote copies, remote signals or barrier semaphores. Data moves between devices by JAX's collectives and lax.ppermute only.
A program may use at most 256 MiB of HBM per device.

v0:
```python
import jax
import jax.numpy as jnp
from jax import lax
from jax.sharding import PartitionSpec as P

ROT = 16


EPSILON = 1e-05


def norm_forward(token_rows, gain_vec, offset):
    row_mean = jnp.mean(token_rows, -1, keepdims=True)
    centered = token_rows - row_mean
    inverse = lax.rsqrt(jnp.mean(centered * centered, -1, keepdims=True) + EPSILON)
    normed = centered * inverse
    return (normed * gain_vec + offset, normed, inverse)


def norm_backward(grad_out, normed, inverse, gain_vec):
    scaled = grad_out * gain_vec
    inner_sum = jnp.mean(scaled * normed, -1, keepdims=True)
    grad_in = inverse * (scaled - jnp.mean(scaled, -1, keepdims=True) - normed * inner_sum)
    return (grad_in, jnp.sum(grad_out * normed, 0), jnp.sum(grad_out, 0))


def rope_tables(places):
    half_rot = ROT // 2
    frequency = 10000.0 ** (-(jnp.arange(half_rot, dtype=jnp.float32) * 2.0) / ROT)
    angles = places.astype(jnp.float32)[:, None] * frequency[None, :]
    return (jnp.cos(angles), jnp.sin(angles))


def rotate(values_in, cosine, sine_tab):
    half_rot = ROT // 2
    first_part = values_in[..., :half_rot]
    second_part = values_in[..., half_rot:ROT]
    return jnp.concatenate(
        [
            first_part * cosine - second_part * sine_tab,
            second_part * cosine + first_part * sine_tab,
            values_in[..., ROT:],
        ],
        -1,
    )


def times_transposed(matrix_a, matrix_b):
    return lax.dot_general(
        matrix_a, matrix_b, (((1,), (1,)), ((), ())), preferred_element_type=jnp.float32
    )


def transposed_times(matrix_a, matrix_b):
    return lax.dot_general(
        matrix_a, matrix_b, (((0,), (0,)), ((), ())), preferred_element_type=jnp.float32
    )


def block_mask(seg_query, index_query, segments_all, block_start, block_end, key_end):
    key_index = jnp.arange(key_end, dtype=jnp.int32)
    same_doc = seg_query[block_start:block_end][:, None] == segments_all[None, :key_end]
    earlier = key_index[None, :] <= index_query[block_start:block_end][:, None]
    return (same_doc & earlier)[:, None, :]


def attend_forward(queries, keys_all, values_all, seg_query, index_query, segments_all):
    row_count = queries.shape[0]
    head_dim = keys_all.shape[1]
    heads_here = queries.shape[1] // head_dim
    full_len = keys_all.shape[0]
    block_rows = 512
    scale_factor = head_dim ** (-0.5)
    outputs, lse_list = ([], [])
    for block_start in range(0, row_count, block_rows):
        block_end = block_start + block_rows
        key_end = min(full_len, block_end)
        query_block = queries[block_start:block_end].reshape(block_rows, heads_here, head_dim)
        scores = (
            jnp.einsum(
                "qhd,kd->qhk", query_block, keys_all[:key_end], preferred_element_type=jnp.float32
            )
            * scale_factor
        )
        allowed = block_mask(seg_query, index_query, segments_all, block_start, block_end, key_end)
        masked = jnp.where(allowed, scores, -1e30)
        top_score = jnp.max(masked, -1, keepdims=True)
        exponent = jnp.exp(masked - top_score)
        total_weight = jnp.sum(exponent, -1, keepdims=True)
        weights_blk = (exponent / total_weight).astype(jnp.bfloat16)
        out_block = jnp.einsum(
            "qhk,kd->qhd", weights_blk, values_all[:key_end], preferred_element_type=jnp.float32
        )
        outputs.append(out_block.reshape(block_rows, heads_here * head_dim).astype(jnp.bfloat16))
        lse_list.append(top_score + jnp.log(total_weight))
    return (jnp.concatenate(outputs, 0), lse_list)


def attend_backward(
    queries, keys_all, values_all, grad_heads, lse_list, seg_query, index_query, segments_all
):
    row_count = queries.shape[0]
    head_dim = keys_all.shape[1]
    heads_here = queries.shape[1] // head_dim
    full_len = keys_all.shape[0]
    block_rows = 512
    scale_factor = head_dim ** (-0.5)
    grad_query_parts = []
    grad_kv = jnp.zeros((full_len, 2 * head_dim), jnp.float32)
    for block_number, block_start in enumerate(range(0, row_count, block_rows)):
        block_end = block_start + block_rows
        key_end = min(full_len, block_end)
        query_block = queries[block_start:block_end].reshape(block_rows, heads_here, head_dim)
        grad_block = grad_heads[block_start:block_end].reshape(block_rows, heads_here, head_dim)
        scores = (
            jnp.einsum(
                "qhd,kd->qhk", query_block, keys_all[:key_end], preferred_element_type=jnp.float32
            )
            * scale_factor
        )
        allowed = block_mask(seg_query, index_query, segments_all, block_start, block_end, key_end)
        masked = jnp.where(allowed, scores, -1e30)
        probs_f = jnp.exp(masked - lse_list[block_number])
        weights_blk = probs_f.astype(jnp.bfloat16)
        grad_weights = jnp.einsum(
            "qhd,kd->qhk", grad_block, values_all[:key_end], preferred_element_type=jnp.float32
        )
        row_inner = jnp.sum(probs_f * grad_weights, -1, keepdims=True)
        grad_scores = (probs_f * (grad_weights - row_inner)).astype(jnp.bfloat16)
        grad_query_block = (
            jnp.einsum(
                "qhk,kd->qhd", grad_scores, keys_all[:key_end], preferred_element_type=jnp.float32
            )
            * scale_factor
        )
        grad_key_part = (
            jnp.einsum("qhk,qhd->kd", grad_scores, query_block, preferred_element_type=jnp.float32)
            * scale_factor
        )
        grad_value_part = jnp.einsum(
            "qhk,qhd->kd", weights_blk, grad_block, preferred_element_type=jnp.float32
        )
        grad_kv = grad_kv.at[:key_end].add(jnp.concatenate([grad_key_part, grad_value_part], 1))
        grad_query_parts.append(grad_query_block.reshape(block_rows, heads_here * head_dim))
    return (jnp.concatenate(grad_query_parts, 0), grad_kv)


def gelu_exact(values_in):
    return jax.nn.gelu(values_in, approximate=False)


def one_row(
    token_in,
    grad_in_row,
    segments,
    places_full,
    norm1_gain,
    norm1_bias,
    norm2_gain,
    norm2_bias,
    query_weight,
    query_bias,
    key_weight,
    key_bias,
    value_weight,
    value_bias,
    output_weight,
    output_bias,
    hidden_weight,
    hidden_bias,
    down_weight,
    down_bias,
):
    sp_count = lax.axis_size("sp")
    local_len = token_in.shape[0]
    model_width = token_in.shape[1]
    head_dim = key_weight.shape[1]
    rot_dims = key_bias.shape[0]
    heads_all = model_width // head_dim
    full_len = local_len * sp_count
    start_row = lax.axis_index("sp") * local_len
    places_local = lax.dynamic_slice_in_dim(places_full, start_row, local_len)
    cos_local, sin_local = rope_tables(places_local)
    full_index = jnp.arange(full_len, dtype=jnp.int32)
    token_rows = token_in.astype(jnp.float32)
    norm_one, normed_one, inverse_one = norm_forward(
        token_rows, norm1_gain.astype(jnp.float32), norm1_bias.astype(jnp.float32)
    )
    attn_input = norm_one.astype(jnp.bfloat16)
    key_shift = jnp.concatenate(
        [key_bias.astype(jnp.float32), jnp.zeros((head_dim - rot_dims,), jnp.float32)]
    )
    query_pre = jnp.dot(
        attn_input, query_weight, preferred_element_type=jnp.float32
    ) + query_bias.astype(jnp.float32)
    key_pre = jnp.dot(attn_input, key_weight, preferred_element_type=jnp.float32) + key_shift
    value_pre = jnp.dot(
        attn_input, value_weight, preferred_element_type=jnp.float32
    ) + value_bias.astype(jnp.float32)
    query_rot = rotate(
        query_pre.reshape(local_len, heads_all, head_dim),
        cos_local[:, None, :],
        sin_local[:, None, :],
    )
    query_rot = query_rot.reshape(local_len, model_width).astype(jnp.bfloat16)
    key_rot = rotate(key_pre, cos_local, sin_local).astype(jnp.bfloat16)
    kv_local = jnp.concatenate([key_rot, value_pre.astype(jnp.bfloat16)], 1)
    kv_full = lax.all_gather(kv_local, "sp", axis=0, tiled=True)
    keys_all = kv_full[:, :head_dim]
    values_all = kv_full[:, head_dim:]
    queries = lax.all_to_all(query_rot, "sp", split_axis=1, concat_axis=0, tiled=True)
    heads_out, lse_list = attend_forward(
        queries, keys_all, values_all, segments, full_index, segments
    )
    attn_local = lax.all_to_all(heads_out, "sp", split_axis=0, concat_axis=1, tiled=True)
    attn_branch = jnp.dot(
        attn_local, output_weight, preferred_element_type=jnp.float32
    ) + output_bias.astype(jnp.float32)
    norm_two, normed_two, inverse_two = norm_forward(
        token_rows, norm2_gain.astype(jnp.float32), norm2_bias.astype(jnp.float32)
    )
    mlp_input = norm_two.astype(jnp.bfloat16)
    pre_act = jnp.dot(
        mlp_input, hidden_weight, preferred_element_type=jnp.float32
    ) + hidden_bias.astype(jnp.float32)
    activated, gelu_pull = jax.vjp(gelu_exact, pre_act)
    act_low = activated.astype(jnp.bfloat16)
    mlp_branch = jnp.dot(
        act_low, down_weight, preferred_element_type=jnp.float32
    ) + down_bias.astype(jnp.float32)
    layer_row = (token_rows + attn_branch + mlp_branch).astype(jnp.bfloat16)
    grad_rows_f = grad_in_row.astype(jnp.float32)
    grad_act = times_transposed(grad_in_row, down_weight)
    grad_pre_low = gelu_pull(grad_act)[0].astype(jnp.bfloat16)
    down_weight_grad = transposed_times(act_low, grad_in_row)
    down_bias_grad = jnp.sum(grad_rows_f, 0)
    hidden_weight_grad = transposed_times(mlp_input, grad_pre_low)
    hidden_bias_grad = jnp.sum(grad_pre_low.astype(jnp.float32), 0)
    grad_norm_two = times_transposed(grad_pre_low, hidden_weight)
    mlp_back, norm2_gain_grad, norm2_bias_grad = norm_backward(
        grad_norm_two, normed_two, inverse_two, norm2_gain.astype(jnp.float32)
    )
    grad_attn_low = times_transposed(grad_in_row, output_weight).astype(jnp.bfloat16)
    output_weight_grad = transposed_times(attn_local, grad_in_row)
    grad_heads = lax.all_to_all(grad_attn_low, "sp", split_axis=1, concat_axis=0, tiled=True)
    grad_queries, grad_kv = attend_backward(
        queries, keys_all, values_all, grad_heads, lse_list, segments, full_index, segments
    )
    cos_full, sin_full = rope_tables(places_full)
    heads_here = grad_queries.shape[1] // head_dim
    grad_query_full = rotate(
        grad_queries.reshape(full_len, heads_here, head_dim),
        cos_full[:, None, :],
        -sin_full[:, None, :],
    )
    grad_query_full = grad_query_full.reshape(full_len, heads_here * head_dim).astype(jnp.bfloat16)
    grad_query_local = lax.all_to_all(
        grad_query_full, "sp", split_axis=0, concat_axis=1, tiled=True
    )
    grad_kv_local = lax.psum_scatter(grad_kv, "sp", scatter_dimension=0, tiled=True)
    grad_key_low = rotate(grad_kv_local[:, :head_dim], cos_local, -sin_local).astype(jnp.bfloat16)
    grad_value_low = grad_kv_local[:, head_dim:].astype(jnp.bfloat16)
    query_weight_grad = transposed_times(attn_input, grad_query_local)
    query_bias_grad = jnp.sum(grad_query_local.astype(jnp.float32), 0)
    key_weight_grad = transposed_times(attn_input, grad_key_low)
    key_bias_grad = jnp.sum(grad_key_low[:, :rot_dims].astype(jnp.float32), 0)
    value_weight_grad = transposed_times(attn_input, grad_value_low)
    value_bias_grad = jnp.sum(grad_value_low.astype(jnp.float32), 0)
    grad_norm_one = (
        times_transposed(grad_query_local, query_weight)
        + times_transposed(grad_key_low, key_weight)
        + times_transposed(grad_value_low, value_weight)
    )
    attn_back, norm1_gain_grad, norm1_bias_grad = norm_backward(
        grad_norm_one, normed_one, inverse_one, norm1_gain.astype(jnp.float32)
    )
    input_row = grad_rows_f + attn_back + mlp_back
    grad_list = [
        norm1_gain_grad,
        norm1_bias_grad,
        norm2_gain_grad,
        norm2_bias_grad,
        query_weight_grad,
        query_bias_grad,
        key_weight_grad,
        key_bias_grad,
        value_weight_grad,
        value_bias_grad,
        output_weight_grad,
        down_bias_grad,
        hidden_weight_grad,
        hidden_bias_grad,
        down_weight_grad,
        down_bias_grad,
    ]
    return (layer_row, input_row, grad_list)


def on_device(
    inputs,
    out_grad,
    segment_ids,
    positions,
    norm1_gain,
    norm1_bias,
    norm2_gain,
    norm2_bias,
    query_weight,
    query_bias,
    key_weight,
    key_bias,
    value_weight,
    value_bias,
    output_weight,
    output_bias,
    hidden_weight,
    hidden_bias,
    down_weight,
    down_bias,
):
    sp_count = lax.axis_size("sp")
    params_all = (
        norm1_gain,
        norm1_bias,
        norm2_gain,
        norm2_bias,
        query_weight,
        query_bias,
        key_weight,
        key_bias,
        value_weight,
        value_bias,
        output_weight,
        output_bias,
        hidden_weight,
        hidden_bias,
        down_weight,
        down_bias,
    )
    layer_rows, input_rows = ([], [])
    grad_list = None
    for row_number in range(inputs.shape[0]):
        layer_row, input_row, row_grads = one_row(
            inputs[row_number],
            out_grad[row_number],
            segment_ids[row_number],
            positions[row_number],
            *params_all
        )
        layer_rows.append(layer_row)
        input_rows.append(input_row)
        if grad_list is None:
            grad_list = row_grads
        else:
            grad_list = [total + part for total, part in zip(grad_list, row_grads)]
    layer_out = jnp.stack(layer_rows, 0)
    input_grad = jnp.stack(input_rows, 0)
    flat_parts = [each_grad.reshape(sp_count, -1) for each_grad in grad_list]
    part_sizes = [piece.shape[1] for piece in flat_parts]
    packed = jnp.concatenate(flat_parts, 1)
    own_row = lax.psum_scatter(packed, "sp", scatter_dimension=0, tiled=True)
    summed = lax.psum(own_row, "dp").reshape(-1)
    results = []
    offset_now = 0
    for each_grad, size_now in zip(grad_list, part_sizes):
        shard_shape = (each_grad.shape[0] // sp_count,) + each_grad.shape[1:]
        results.append(summed[offset_now : offset_now + size_now].reshape(shard_shape))
        offset_now = offset_now + size_now
    return (layer_out, input_grad) + tuple(results)


def solution(mesh):
    placed = (
        P("dp", "sp", None),
        P("dp", "sp", None),
        P("dp", None),
        P("dp", None),
        P(),
        P(),
        P(),
        P(),
        P(),
        P(),
        P(),
        P(),
        P(),
        P(),
        P(),
        P(),
        P(),
        P(),
        P(),
        P(),
    )
    return jax.shard_map(
        on_device,
        mesh=mesh,
        in_specs=placed,
        out_specs=(
            P("dp", "sp", None),
            P("dp", "sp", None),
            P("sp"),
            P("sp"),
            P("sp"),
            P("sp"),
            P("sp", None),
            P("sp"),
            P("sp", None),
            P("sp"),
            P("sp", None),
            P("sp"),
            P("sp", None),
            P("sp"),
            P("sp", None),
            P("sp"),
            P("sp", None),
            P("sp"),
        ),
        check_vma=False,
    )
```

profile of v0, /device:TPU:0, one launch (start us, length us, event | category | flops | bytes accessed | tf_op | source)
XLA Modules:
  0.0 1696.9 jit_solution(9105256135938720582)
XLA Ops:
  10.8 6.3 all-to-all-start.4
  46.2 16.8 all_gather.7
  77.7 34.7 %multiply_convert_fusion.7 = (bf16[512,3072]{1,0:T(8,128)(2,1)}, f32[512,3072]{1,0:T(8,128)}, bf16[512,3072]{1,0:T(8,128)(2,1)}, f32[512,3072]{1,0:T(8,128)}, f32[512,3072]{1,0:T(8,128)}) fusion(f32[3072]{0:T(1024)S(1)} %copy-done.121, f32[512,3072]{1,0:T(8,128)S(1)} %fusion.278, bf16[768,3072]{1,0:T(8,128)(2,1)S(1)} %bitcast.595, ...), kind=kOutput, calls=%fused_computation.66 | convolution fusion | flops 2625896448 | bytes 36986880 | tf_op jit(solution)/shard_map/dot_general | solution.py:223
  112.5 7.6 convert_reduce_fusion
  120.0 9.0 convert_reduce_fusion.1
  140.2 14.0 reshape.1321
  164.4 12.0 reshape.1322
  190.6 6.2 fusion.307
  202.3 27.9 %all_gather.6 = bf16[2048,128]{0,1:T(8,128)(2,1)S(1)} all-gather(bf16[512,128]{0,1:T(8,128)(2,1)S(1)} %pad_maximum_fusion.10), channel_id=1, replica_groups=mesh['dp'=8,'sp'=4] {'sp'}, dimensions={0}, use_global_device_ids=true | all-gather | bytes 655360 | tf_op jit(solution)/shard_map/all_gather | solution.py:208
  230.2 7.1 fusion.305
  252.7 7.2 all-to-all-done.2
  271.1 9.9 all-to-all-done.6
  363.8 6.4 fusion
  370.3 7.8 fusion.157
  381.5 8.6 multiply_reduce_fusion.1
  390.1 9.4 multiply_convert_fusion.1
  410.2 6.5 multiply_convert_fusion
  438.3 8.3 all-to-all-done.3
  464.2 6.2 fusion.59
  470.6 6.7 all-to-all-done.1
  490.3 7.5 fusion.67
  520.3 16.7 all-to-all-done.7
  610.2 13.7 dynamic-update-slice.32
  625.4 49.6 %dynamic-update-slice.34 = f32[4,1501268]{1,0:T(4,128)} dynamic-update-slice(f32[4,1501268]{1,0:T(4,128)} %dynamic-update-slice.33, f32[4,589824]{1,0:T(4,128)} %reshape.1321, s32[]{} %constant.345, s32[]{} %constant.357) | dynamic-update-slice | bytes 18874372
  676.5 49.2 %dynamic-update-slice.36 = f32[4,1501268]{1,0:T(4,128)} dynamic-update-slice(f32[4,1501268]{1,0:T(4,128)} %dynamic-update-slice.35, f32[4,589824]{1,0:T(4,128)} %reshape.1322, s32[]{} %constant.345, s32[]{} %constant.359) | dynamic-update-slice | bytes 18874372
  728.4 7.1 fusion.302
  735.5 788.8 %all-reduce.9.cloned.1.call-done = f32[4,1501268]{1,0:T(4,128)} async-done(((f32[4,1501268]{1,0:T(4,128)}), f32[4,1501268]{1,0:T(4,128)}) %all-reduce.9.cloned.1.call-update) | async-done | bytes 24020304
  1524.2 12.7 constant_dynamic-slice_fusion
  1536.9 6.0 fusion.303
  1551.1 86.1 %all-reduce.7.cloned.1.call-done = f32[1,1501268]{1,0:T(1,128)} async-done(((f32[1,1501268]{1,0:T(1,128)}), f32[1,1501268]{1,0:T(1,128)}) %all-reduce.7.cloned.1.call-update) | async-done | bytes 6005088 | tf_op jit(solution)/shard_map/psum | solution.py:362
  1640.0 27.6 %slice_reduce_fusion = (f32[589824]{0:T(1024)}, f32[589824]{0:T(1024)S(1)}) fusion(f32[1,1501268]{1,0:T(1,128)} %all-reduce.7.cloned.1.call-done), kind=kLoop, calls=%fused_computation.133 | loop fusion | bytes 9437184 | tf_op jit(solution)/shard_map/slice | solution.py:367
  1670.9 8.6 slice_reduce_fusion.2
  (566 shorter events, 389.1 us)
Async XLA Ops:
  7.2 26.2 %copy-start = (bf16[768,768]{1,0:T(8,128)(2,1)S(1)}, bf16[768,768]{1,0:T(8,128)(2,1)}, u32[]{:S(2)}) copy-start(bf16[768,768]{1,0:T(8,128)(2,1)} %param.48) | copy-start | bytes 3538948
  9.6 17.9 %copy-start.9 = (bf16[2,512,768]{2,1,0:T(8,128)(2,1)S(1)}, bf16[2,512,768]{2,1,0:T(8,128)(2,1)}, u32[]{:S(2)}) copy-start(bf16[2,512,768]{2,1,0:T(8,128)(2,1)} %param.40) | copy-start | bytes 4718596
  10.8 186.0 %all-to-all-start.4 = ((bf16[512,4,192]{0,2,1:T(8,128)(2,1)}), bf16[512,4,192]{0,2,1:T(8,128)(2,1)}, u32[]{:S(2)}, u32[]{:S(2)}) async-start(bf16[512,4,192]{0,2,1:T(8,128)(2,1)} %bitcast.61), calls=%async_computation.4 | async-start | bytes 1572864 | tf_op jit(solution)/shard_map/all_to_all | solution.py:245
  27.9 101.8 %copy-start.85 = (f32[512]{0:T(512)}, f32[512]{0:T(512)S(1)}, u32[]{:S(2)}) copy-start(f32[512]{0:T(512)S(1)} %get-tuple-element.347) | copy-start | bytes 6148
  28.5 101.1 %copy-start.90 = (f32[512]{0:T(512)}, f32[512]{0:T(512)S(1)}, u32[]{:S(2)}) copy-start(f32[512]{0:T(512)S(1)} %add_rsqrt_fusion.1) | copy-start | bytes 6148
  37.3 97.3 %copy-start.71 = (f32[768]{0:T(1024)}, f32[768]{0:T(1024)S(1)}, u32[]{:S(2)}) copy-start(f32[768]{0:T(1024)S(1)} %convert_element_type.350) | copy-start | bytes 9220
  44.3 26.9 %copy-start.115 = (f32[1,512]{1,0:T(1,128)}, f32[1,512]{1,0:T(1,128)S(1)}, u32[]{:S(2)}) copy-start(f32[1,512]{1,0:T(1,128)S(1)} %get-tuple-element.348) | copy-start | bytes 6148
  44.3 26.9 %copy-start.117 = (f32[1,512]{1,0:T(1,128)}, f32[1,512]{1,0:T(1,128)S(1)}, u32[]{:S(2)}) copy-start(f32[1,512]{1,0:T(1,128)S(1)} %get-tuple-element.349) | copy-start | bytes 6148
  72.8 39.6 %slice-start.5 = ((s8[4718592]{0:T(1024)(128)(4,1)}), s8[4194304]{0:T(1024)(128)(4,1)S(1)}, s32[]{:S(2)}) async-start(s8[4718592]{0:T(1024)(128)(4,1)} %bitcast.596), calls=%async_computation.19 | async-start | bytes 8388608
  77.7 34.7 %copy-start.14 = (bf16[2,512,768]{2,1,0:T(8,128)(2,1)S(1)}, bf16[2,512,768]{2,1,0:T(8,128)(2,1)}, u32[]{:S(2)}) copy-start(bf16[2,512,768]{2,1,0:T(8,128)(2,1)} %param.41) | copy-start | bytes 4718596
  77.7 34.7 %slice-start.6 = ((s8[4718592]{0:T(1024)(128)(4,1)}), s8[524288]{0:T(1024)(128)(4,1)S(1)}, s32[]{:S(2)}) async-start(s8[4718592]{0:T(1024)(128)(4,1)} %bitcast.596), calls=%async_computation.20 | async-start | bytes 1048576
  196.8 42.6 %all-to-all-start = ((bf16[512,4,192]{0,2,1:T(8,128)(2,1)}), bf16[512,4,192]{0,2,1:T(8,128)(2,1)S(1)}, u32[]{:S(2)}, u32[]{:S(2)}) async-start(bf16[512,4,192]{0,2,1:T(8,128)(2,1)} %bitcast.4), calls=%async_computation | async-start | bytes 1572864 | tf_op jit(solution)/shard_map/all_to_all | solution.py:211
  240.3 19.7 %all-to-all-start.2 = ((bf16[512,4,192]{0,2,1:T(8,128)(2,1)}), bf16[512,4,192]{0,2,1:T(8,128)(2,1)S(1)}, u32[]{:S(2)}, u32[]{:S(2)}) async-start(bf16[512,4,192]{0,2,1:T(8,128)(2,1)} %bitcast.34), calls=%async_computation.2 | async-start | bytes 1572864 | tf_op jit(solution)/shard_map/all_to_all | solution.py:211
  259.9 21.1 %all-to-all-start.6 = ((bf16[512,4,192]{0,2,1:T(8,128)(2,1)}), bf16[512,4,192]{0,2,1:T(8,128)(2,1)}, u32[]{:S(2)}, u32[]{:S(2)}) async-start(bf16[512,4,192]{0,2,1:T(8,128)(2,1)} %bitcast.80), calls=%async_computation.7 | async-start | bytes 1572864 | tf_op jit(solution)/shard_map/all_to_all | solution.py:245
  267.2 18.8 %copy-start.94 = (f32[512,3]{0,1:T(4,128)}, f32[512,3]{0,1:T(4,128)S(1)}, u32[]{:S(2)}) copy-start(f32[512,3]{0,1:T(4,128)S(1)} %log_add_fusion.3) | copy-start | bytes 18436
  283.2 24.8 %copy-start.40 = (bf16[1,512,192]{1,2,0:T(8,128)(2,1)}, bf16[1,512,192]{1,2,0:T(8,128)(2,1)S(1)}, u32[]{:S(2)}) copy-start(bf16[1,512,192]{1,2,0:T(8,128)(2,1)S(1)} %get-tuple-element.249) | copy-start | bytes 589828
  290.7 18.8 %copy-start.3 = (f32[512,3,1024]{2,0,1:T(8,128)}, f32[512,3,1024]{2,0,1:T(8,128)S(1)}, u32[]{:S(2)}) copy-start(f32[512,3,1024]{2,0,1:T(8,128)S(1)} %get-tuple-element.314) | copy-start | bytes 18874372
  292.3 17.3 %copy-start.92 = (f32[512,3]{0,1:T(4,128)}, f32[512,3]{0,1:T(4,128)S(1)}, u32[]{:S(2)}) copy-start(f32[512,3]{0,1:T(4,128)S(1)} %log_add_fusion.2) | copy-start | bytes 18436
  316.2 27.9 %copy-start.2 = (f32[512,3,1536]{2,0,1:T(8,128)}, f32[512,3,1536]{2,0,1:T(8,128)S(1)}, u32[]{:S(2)}) copy-start(f32[512,3,1536]{2,0,1:T(8,128)S(1)} %get-tuple-element.312) | copy-start | bytes 28311556
  353.1 57.2 %copy-start.1 = (f32[512,3,2048]{2,0,1:T(8,128)}, f32[512,3,2048]{2,0,1:T(8,128)S(1)}, u32[]{:S(2)}) copy-start(f32[512,3,2048]{2,0,1:T(8,128)S(1)} %get-tuple-element.310) | copy-start | bytes 37748740
  422.5 24.0 %all-to-all-start.3 = ((bf16[4,512,192]{1,2,0:T(8,128)(2,1)}), bf16[4,512,192]{1,2,0:T(8,128)(2,1)S(1)}, u32[]{:S(2)}, u32[]{:S(2)}) async-start(bf16[4,512,192]{1,2,0:T(8,128)(2,1)} %bitcast.510), calls=%async_computation.3 | async-start | bytes 1572864 | tf_op jit(solution)/shard_map/all_to_all | solution.py:215
  426.2 128.1 %reduce-scatter.3.cloned.1.call-start = ((), (), s32[]{:S(2)}) async-start(), calls=%async_computation.10 | async-start | bytes 1310720 | tf_op jit(solution)/shard_map/reduce_scatter | solution.py:260
  437.5 22.6 %copy-start.93 = (f32[512,3]{0,1:T(4,128)S(1)}, f32[512,3]{0,1:T(4,128)}, u32[]{:S(2)}) copy-start(f32[512,3]{0,1:T(4,128)} %copy-done.92) | copy-start | bytes 18436
  446.6 17.7 %copy-start.28 = (bf16[4,512,192]{1,2,0:T(8,128)(2,1)}, bf16[4,512,192]{1,2,0:T(8,128)(2,1)S(1)}, u32[]{:S(2)}) copy-start(bf16[4,512,192]{1,2,0:T(8,128)(2,1)S(1)} %all-to-all-done.3) | copy-start | bytes 2359300
  446.6 30.7 %all-to-all-start.1 = ((bf16[4,512,192]{1,2,0:T(8,128)(2,1)}), bf16[4,512,192]{1,2,0:T(8,128)(2,1)}, u32[]{:S(2)}, u32[]{:S(2)}) async-start(bf16[4,512,192]{1,2,0:T(8,128)(2,1)} %bitcast.526), calls=%async_computation.1 | async-start | bytes 1572864 | tf_op jit(solution)/shard_map/all_to_all | solution.py:215
  477.3 23.3 %all-to-all-start.5 = ((bf16[4,512,192]{1,2,0:T(8,128)(2,1)}), bf16[4,512,192]{1,2,0:T(8,128)(2,1)S(1)}, u32[]{:S(2)}, u32[]{:S(2)}) async-start(bf16[4,512,192]{1,2,0:T(8,128)(2,1)} %copy.106), calls=%async_computation.5 | async-start | bytes 1572864 | tf_op jit(solution)/shard_map/all_to_all | solution.py:257
  501.5 35.5 %all-to-all-start.7 = ((bf16[4,512,192]{1,2,0:T(8,128)(2,1)}), bf16[4,512,192]{1,2,0:T(8,128)(2,1)S(1)}, u32[]{:S(2)}, u32[]{:S(2)}) async-start(bf16[4,512,192]{1,2,0:T(8,128)(2,1)} %copy.111), calls=%async_computation.8 | async-start | bytes 1572864 | tf_op jit(solution)/shard_map/all_to_all | solution.py:257
  505.0 53.6 %reduce-scatter.5.cloned.1.call-start = ((), (), s32[]{:S(2)}) async-start(), calls=%async_computation.11 | async-start | bytes 1310720 | tf_op jit(solution)/shard_map/reduce_scatter | solution.py:260
  507.7 1016.6 %all-reduce.9.cloned.1.call-start = ((), (), s32[]{:S(2)}) async-start(), calls=%async_computation.13 | async-start | bytes 48041984
  512.5 24.5 %copy-start.100 = (f32[512]{0:T(512)S(1)}, f32[512]{0:T(512)}, u32[]{:S(2)}) copy-start(f32[512]{0:T(512)} %copy-done.98) | copy-start | bytes 6148
  625.4 49.6 %copy-start.105 = (f32[4,768]{1,0:T(4,128)S(1)}, f32[4,768]{1,0:T(4,128)}, u32[]{:S(2)}) copy-start(f32[4,768]{1,0:T(4,128)} %add.500) | copy-start | bytes 36868
  727.2 910.0 %all-reduce.7.cloned.1.call-start = ((), (), s32[]{:S(2)}) async-start(), calls=%async_computation.12 | async-start | bytes 12010496 | tf_op jit(solution)/shard_map/psum | solution.py:362
  (130 other events, 772.2 us)
Sparse Core Ops, SparseCore 0:
  432.3 37.6 reduce-scatter.2
  508.2 33.9 reduce-scatter.4
  727.3 796.9 all-reduce.8
  1537.0 100.1 all-reduce.6
where the time goes:
time: 1710 us; the launch traced here: 1700 us
  waiting for transfers between devices  927 us (54%)
  local copies, waits for them, and re-layouts  289 us (17%)
  matrix products  281 us (16%)
  other arithmetic  104 us (6%)
  blocking collectives  44.7 us (3%)
  starting transfers between devices  35.8 us (2%)
    unnamed x5, waiting for transfers between devices  789 us
    unnamed x319, local copies, waits for them, and re-layouts  155 us
    psum x1, waiting for transfers between devices, on_device(): summed = lax.psum(own_row, 'dp').reshape(-1)  86.1 us
    dot_general x12, matrix products, times_transposed(): lax.dot_general(matrix_a, matrix_b, (((1,), (1,)), ((), ())), preferred_e...  53.4 us
    all_gather x2, blocking collectives, one_row(): kv_full = lax.all_gather(kv_local, 'sp', axis=0, tiled=True)  44.7 us
    slice x7, local copies, waits for them, and re-layouts, on_device(): summed[offset_now:offset_now + size_now].reshape(shard_shape)  42.4 us
    dot_general x12, matrix products, transposed_times(): lax.dot_general(matrix_a, matrix_b, (((0,), (0,)), ((), ())), preferred_e...  41 us
    dot_general x2, matrix products, one_row(): jnp.dot(mlp_input, hidden_weight, preferred_element_type=jnp.float32)  39.5 us
  transfers between devices with their start and end apart: 12, of which 8 were waited for; matrix products, arithmetic and copies ran while one was open for 17% of the time, Pallas kernels for 0%

commit v1 on v0

v1 whole, which is shorter than its diff:
```python
import functools, jax, jax.numpy as jnp
from jax import lax
from jax.experimental import pallas as pl
from jax.experimental.pallas import tpu as pltpu
EPS=1e-5
NT=(((1,),(1,)),((),()))
TN=(((0,),(0,)),((),()))
def dotf(a,b,dims=(((1,),(0,)),((),()))):
    return lax.dot_general(a,b,dims,preferred_element_type=jnp.float32)
def ln(xv):
    m=jnp.mean(xv,-1,keepdims=True); c=xv-m
    s=lax.rsqrt(jnp.mean(c*c,-1,keepdims=True)+EPS)
    return c*s, s
C1=0.7071067811865476; C2=0.3989422804014327
def mlp_kernel(x_ref,g_ref,w1_ref,w2_ref,b1_ref,gain_ref,bias_ref,
               br_ref,dm_ref,dw1_ref,dw2_ref,db1_ref, mi_ref,mit_ref,act_ref,gp_ref,*,rows):
    j=pl.program_id(0)
    N=x_ref.shape[0]
    @pl.when(j==0)
    def _():
        for r in range(0,N,256):
            n,_s=ln(x_ref[r:r+256,:].astype(jnp.float32))
            mi=(n*gain_ref[...]+bias_ref[...])
            mi_ref[r:r+256,:]=mi.astype(jnp.bfloat16)
            mit_ref[:,r:r+256]=mi.astype(jnp.bfloat16).T
        br_ref[...]=jnp.zeros_like(br_ref); dm_ref[...]=jnp.zeros_like(dm_ref)
    w1=w1_ref[...]; w2=w2_ref[...]; b1=b1_ref[...]
    db=jnp.zeros((1,w1.shape[1]),jnp.float32)
    for r in range(0,N,rows):
        sl=slice(r,r+rows)
        pre=dotf(mi_ref[sl,:],w1)+b1
        da=dotf(g_ref[sl,:],w2,NT)
        phi=0.5*(1.0+lax.erf(pre*C1))
        act=(pre*phi).astype(jnp.bfloat16)
        dg=phi+pre*(jnp.exp(pre*pre*-0.5)*C2)
        gp=(da*dg).astype(jnp.bfloat16)
        act_ref[sl,:]=act
        gp_ref[sl,:]=gp
        db=db+jnp.sum(gp.astype(jnp.float32),0,keepdims=True)
        br_ref[sl,:]+=dotf(act,w2)
        dm_ref[sl,:]+=dotf(gp,w1,NT)
    db1_ref[...]=db
    dw1_ref[...]=dotf(mit_ref[...],gp_ref[...]).astype(dw1_ref.dtype)
    dw2_ref[...]=dotf(act_ref[...],g_ref[...],TN).astype(dw2_ref.dtype)

def mlp(x,g,w1,w2,b1,gain,bias,bw=256,rows=256):
    N,D=x.shape; F=w1.shape[1]
    n=F//bw
    full=lambda s: pl.BlockSpec(s,lambda j:(0,0))
    return pl.pallas_call(functools.partial(mlp_kernel,rows=rows),
      grid=(n,),
      in_specs=[full((N,D)),full((N,D)),pl.BlockSpec((D,bw),lambda j:(0,j)),pl.BlockSpec((bw,D),lambda j:(j,0)),
                pl.BlockSpec((1,bw),lambda j:(0,j)),full((1,D)),full((1,D))],
      out_specs=[full((N,D)),full((N,D)),pl.BlockSpec((D,bw),lambda j:(0,j)),pl.BlockSpec((bw,D),lambda j:(j,0)),pl.BlockSpec((1,bw),lambda j:(0,j))],
      out_shape=[jax.ShapeDtypeStruct((N,D),jnp.float32)]*2+[jax.ShapeDtypeStruct((D,F),jnp.bfloat16),jax.ShapeDtypeStruct((F,D),jnp.bfloat16),jax.ShapeDtypeStruct((1,F),jnp.float32)],
      scratch_shapes=[pltpu.VMEM((N,D),jnp.bfloat16),pltpu.VMEM((D,N),jnp.bfloat16),pltpu.VMEM((N,bw),jnp.bfloat16),pltpu.VMEM((N,bw),jnp.bfloat16)],
      compiler_params=pltpu.CompilerParams(dimension_semantics=("arbitrary",),vmem_limit_bytes=56<<20),
      name="mlp")(x,g,w1,w2,b1,gain,bias)
def lane_iota(shape):
    return lax.broadcasted_iota(jnp.int32,shape,len(shape)-1)
def rope_apply(v,C,S,sign):
    l=lane_iota(v.shape)%64
    sh=jnp.where(l<8,pltpu.roll(v,120,1),jnp.where(l<16,pltpu.roll(v,8,1),0.0))
    return v*C+(sh*S if sign>0 else -(sh*S))
def pre_kernel(x_ref,g_ref,cs_ref,wq_ref,wkv_ref,wo_ref,bq_ref,bkv_ref,gain_ref,bias_ref,
               q_ref,kv_ref,do_ref,tab_ref):
    n,_=ln(x_ref[...].astype(jnp.float32))
    ai=(n*gain_ref[...]+bias_ref[...]).astype(jnp.bfloat16)
    B=ai.shape[0]
    t=cs_ref[...]
    t=jnp.concatenate([t,jnp.zeros((128-t.shape[0],B),jnp.float32)],0).T
    l=lane_iota((B,128))
    co=jnp.where(l<8,t,0.0)
    c2=co+pltpu.roll(co,8,1)
    C=c2+pltpu.roll(c2,64,1)+jnp.where(l%64>=16,1.0,0.0)
    sb=jnp.where((l>=8)&(l<16),t,0.0)
    s2=sb-pltpu.roll(sb,120,1)
    S=s2+pltpu.roll(s2,64,1)
    tab_ref[:,:128]=C
    ds=pltpu.roll(t,111,1)
    tab_ref[:,128:]=jnp.where(l==127,ds,S)
    q=dotf(ai,wq_ref[...])+bq_ref[...]
    for c in range(0,q.shape[1],128):
        q_ref[:,c:c+128]=(rope_apply(q[:,c:c+128],C,S,1)*0.125).astype(jnp.bfloat16)
    kv=dotf(ai,wkv_ref[...])+bkv_ref[...]
    kv_ref[...]=rope_apply(kv,jnp.where(l<64,C,1.0),jnp.where(l<64,S,0.0),1).astype(jnp.bfloat16)
    do_ref[...]=dotf(g_ref[...],wo_ref[...],NT).astype(jnp.bfloat16)
def pre(x,g,cs,wq,wkv,wo,bq,bkv,gain,bias,B=256):
    N,D=x.shape
    f=lambda a: pl.BlockSpec(a.shape,lambda j:(0,0))
    row=lambda w: pl.BlockSpec((B,w),lambda j:(j,0))
    return pl.pallas_call(pre_kernel,grid=(N//B,),
      in_specs=[row(D),row(D),pl.BlockSpec((cs.shape[0],B),lambda j:(0,j)),f(wq),f(wkv),f(wo),f(bq),f(bkv),f(gain),f(bias)],
      out_specs=[row(D),row(128),row(D),row(256)],
      out_shape=[jax.ShapeDtypeStruct((N,D),jnp.bfloat16),jax.ShapeDtypeStruct((N,128),jnp.bfloat16),jax.ShapeDtypeStruct((N,D),jnp.bfloat16),jax.ShapeDtypeStruct((N,256),jnp.float32)],
      compiler_params=pltpu.CompilerParams(dimension_semantics=("arbitrary",),vmem_limit_bytes=48<<20),name="pre")(x,g,cs,wq,wkv,wo,bq,bkv,gain,bias)

NEG=-1e30
def attn_kernel(p0_ref,q_ref,do_ref,kv_ref,kvp_ref,tab_ref,o_ref,dq_ref,dkv_ref,kx_ref,bias_ref,*,QB):
    r=pl.program_id(0); hp=pl.program_id(1)
    T=q_ref.shape[0]
    @pl.when(hp==0)
    def _():
        for i,ref in enumerate((kvp_ref,kv_ref)):
            kv=ref[...].astype(jnp.float32)
            l=lane_iota(kv.shape)
            ke=jnp.where(l<64,kv,0.0); vo=jnp.where(l>=64,kv,0.0)
            sl=slice(i*T,(i+1)*T)
            kx_ref[0,sl,:]=ke.astype(jnp.bfloat16)
            kx_ref[1,sl,:]=pltpu.roll(ke,64,1).astype(jnp.bfloat16)
            kx_ref[2,sl,:]=pltpu.roll(vo,64,1).astype(jnp.bfloat16)
            kx_ref[3,sl,:]=vo.astype(jnp.bfloat16)
        ds=tab_ref[:,255:256]
        kk=(lane_iota((T,2*T))-T)
        qi=lax.broadcasted_iota(jnp.int32,(T,2*T),0)
        ok=(kk.astype(jnp.float32)>=ds)&(kk<=qi)
        bias_ref[...]=jnp.where(ok,0.0,NEG)
        dkv_ref[...]=jnp.zeros_like(dkv_ref)
    def run(lo):
        qT=q_ref[...].T; dT=do_ref[...].T
        for qb in range(0,T,QB):
            hi=T+qb+QB
            rs=slice(qb,qb+QB)
            qv=q_ref[rs,:]; dv=do_ref[rs,:]
            bias=bias_ref[rs,lo:hi]
            o=None; dq=None
            for e in (0,1):
                kx=kx_ref[e,lo:hi,:]; vx=kx_ref[2+e,lo:hi,:]
                s=dotf(qv,kx,NT)+bias
                m=jnp.max(s,-1,keepdims=True)
                p=jnp.exp(s-m)
                p=p*(1.0/jnp.sum(p,-1,keepdims=True))
                pb=p.astype(jnp.bfloat16)
                dp=dotf(dv,vx,NT)
                inner=jnp.sum(p*dp,-1,keepdims=True)
                dsc=(p*(dp-inner)).astype(jnp.bfloat16)
                oh=dotf(pb,vx); dh=dotf(dsc,kx)
                o=oh if o is None else o+oh
                dq=dh if dq is None else dq+dh
                h=slice(e*64,e*64+64)
                dkv_ref[0,:64,lo:hi]+=dotf(qT[h,rs],dsc)
                dkv_ref[0,64:,lo:hi]+=dotf(dT[h,rs],pb)
            o_ref[rs,:]=o.astype(jnp.bfloat16)
            dq_ref[rs,:]=rope_apply(dq*0.125,tab_ref[rs,:128],tab_ref[rs,128:],-1).astype(jnp.bfloat16)
    has=p0_ref[r]>0
    @pl.when(has)
    def _(): run(0)
    @pl.when(jnp.logical_not(has))
    def _(): run(T)
def attn(p0,q,do,kv,kvp,tab,T=512,QB=256):
    N,D=q.shape; R=N//T
    hb=pl.BlockSpec((T,128),lambda r,h,p:(r,h)); rb=lambda w: pl.BlockSpec((T,w),lambda r,h,p:(r,0))
    return pl.pallas_call(functools.partial(attn_kernel,QB=QB),
      grid_spec=pltpu.PrefetchScalarGridSpec(num_scalar_prefetch=1,grid=(R,D//128),
        in_specs=[hb,hb,rb(128),rb(128),rb(256)],
        out_specs=[hb,hb,pl.BlockSpec((1,128,2*T),lambda r,h,p:(r,0,0))],
        scratch_shapes=[pltpu.VMEM((4,2*T,128),jnp.bfloat16),pltpu.VMEM((T,2*T),jnp.float32)]),
      out_shape=[jax.ShapeDtypeStruct((N,D),jnp.bfloat16)]*2+[jax.ShapeDtypeStruct((R,128,2*T),jnp.float32)],
      compiler_params=pltpu.CompilerParams(dimension_semantics=("arbitrary","arbitrary"),vmem_limit_bytes=56<<20),name="attn")(p0,q,do,kv,kvp,tab)
def wgrad_kernel(x_ref,g_ref,o_ref,dq_ref,gain_ref,bias_ref,dwq_ref,dwo_ref,qb_ref,ait_ref,ot_ref):
    j=pl.program_id(0); N=x_ref.shape[0]
    @pl.when(j==0)
    def _():
        for r in range(0,N,256):
            n,_s=ln(x_ref[r:r+256,:].astype(jnp.float32))
            ait_ref[:,r:r+256]=(n*gain_ref[...]+bias_ref[...]).astype(jnp.bfloat16).T
            ot_ref[:,r:r+256]=o_ref[r:r+256,:].T
    dq=dq_ref[...]
    dwq_ref[...]=dotf(ait_ref[...],dq).astype(dwq_ref.dtype)
    dwo_ref[...]=dotf(ot_ref[...],g_ref[...]).astype(dwo_ref.dtype)
    qb_ref[...]=jnp.sum(dq.astype(jnp.float32),0,keepdims=True)
def wgrad(x,g,o,dq,gain,bias,bw=256):
    N,D=x.shape
    full=lambda a: pl.BlockSpec(a.shape,lambda j:(0,0))
    col=pl.BlockSpec((N,bw),lambda j:(0,j)); oc=pl.BlockSpec((D,bw),lambda j:(0,j))
    return pl.pallas_call(wgrad_kernel,grid=(D//bw,),
      in_specs=[full(x),col,full(o),col,full(gain),full(bias)],
      out_specs=[oc,oc,pl.BlockSpec((1,bw),lambda j:(0,j))],
      out_shape=[jax.ShapeDtypeStruct((D,D),jnp.bfloat16)]*2+[jax.ShapeDtypeStruct((1,D),jnp.float32)],
      scratch_shapes=[pltpu.VMEM((D,N),jnp.bfloat16)]*2,
      compiler_params=pltpu.CompilerParams(dimension_semantics=("arbitrary",),vmem_limit_bytes=48<<20),name="wgrad")(x,g,o,dq,gain,bias)
def post_kernel(x_ref,g_ref,o_ref,dq_ref,br_ref,dm_ref,dk_ref,dr_ref,tab_ref,wq_ref,wkv_ref,wo_ref,bo_ref,bd_ref,g1_ref,b1_ref,g2_ref,
                lo_ref,ig_ref,sm_ref,dwkv_ref,kvb_ref):
    j=pl.program_id(0)
    @pl.when(j==0)
    def _():
        sm_ref[...]=jnp.zeros_like(sm_ref); dwkv_ref[...]=jnp.zeros_like(dwkv_ref); kvb_ref[...]=jnp.zeros_like(kvb_ref)
    x=x_ref[...].astype(jnp.float32); g=g_ref[...].astype(jnp.float32)
    n,s=ln(x)
    g1=g1_ref[...]; g2=g2_ref[...]
    ai=(n*g1+b1_ref[...]).astype(jnp.bfloat16)
    dkv=(dk_ref[0]+dr_ref[0].astype(jnp.float32)).T
    l=lane_iota(dkv.shape)
    dkv=rope_apply(dkv,jnp.where(l<64,tab_ref[:,:128],1.0),jnp.where(l<64,tab_ref[:,128:],0.0),-1).astype(jnp.bfloat16)
    kvb_ref[...]+=jnp.sum(dkv.astype(jnp.float32),0,keepdims=True)
    dwkv_ref[...]+=dotf(ai,dkv,TN)
    lo_ref[...]=(x+(dotf(o_ref[...],wo_ref[...])+bo_ref[...])+(br_ref[...]+bd_ref[...])).astype(jnp.bfloat16)
    c1=dotf(dq_ref[...],wq_ref[...],NT)+dotf(dkv,wkv_ref[...],NT)
    c2=dm_ref[...]
    u=c1*g1+c2*g2
    ig_ref[...]=g+s*(u-jnp.mean(u,-1,keepdims=True)-n*jnp.mean(u*n,-1,keepdims=True))
    for i,v in enumerate((c1*n,c1,c2*n,c2,g)):
        sm_ref[i:i+1,:]+=jnp.sum(v,0,keepdims=True)
def post(x,g,o,dq,br,dm,dkv,drecv,tab,wq,wkv,wo,bo,bd,g1,b1,g2,B=256,T=512):
    N,D=x.shape; nb=T//B
    f=lambda a: pl.BlockSpec(a.shape,lambda j:(0,)*a.ndim)
    row=lambda w: pl.BlockSpec((B,w),lambda j:(j,0))
    return pl.pallas_call(post_kernel,grid=(N//B,),
      in_specs=[row(D)]*6+[pl.BlockSpec((1,128,B),lambda j:(j//nb,0,nb+j%nb)),pl.BlockSpec((1,128,B),lambda j:(j//nb,0,j%nb)),row(256)]+[f(a) for a in (wq,wkv,wo,bo,bd,g1,b1,g2)],
      out_specs=[row(D),row(D),pl.BlockSpec((8,D),lambda j:(0,0)),pl.BlockSpec((D,128),lambda j:(0,0)),pl.BlockSpec((1,128),lambda j:(0,0))],
      out_shape=[jax.ShapeDtypeStruct((N,D),jnp.bfloat16),jax.ShapeDtypeStruct((N,D),jnp.float32),jax.ShapeDtypeStruct((8,D),jnp.float32),jax.ShapeDtypeStruct((D,128),jnp.float32),jax.ShapeDtypeStruct((1,128),jnp.float32)],
      compiler_params=pltpu.CompilerParams(dimension_semantics=("arbitrary",),vmem_limit_bytes=56<<20),name="post")(x,g,o,dq,br,dm,dkv,drecv,tab,wq,wkv,wo,bo,bd,g1,b1,g2)
from jax.sharding import PartitionSpec as P
ROT=16
def bits_of(n):
    return n.bit_length()-1
def pair_perm(size,bit):
    return [(i,i^(1<<bit)) for i in range(size)]
def halve(G,axis_name,bit,ax):
    n=lax.axis_size(axis_name)
    my=(lax.axis_index(axis_name)>>bit)&1
    send=lax.dynamic_index_in_dim(G,1-my,ax,keepdims=False)
    keep=lax.dynamic_index_in_dim(G,my,ax,keepdims=False)
    recv=lax.ppermute(send,axis_name,pair_perm(n,bit))
    return (keep.astype(jnp.float32)+recv.astype(jnp.float32)).astype(G.dtype)
def double(own,bit):
    n=lax.axis_size("dp")
    my=(lax.axis_index("dp")>>bit)&1
    recv=lax.ppermute(own,"dp",pair_perm(n,bit))
    buf=jnp.stack([own,own])
    return lax.dynamic_update_index_in_dim(buf,recv,1-my,0)
def reduce_stream(G,order):
    sp=lax.axis_size("sp"); nb=len(order); rows=G.shape[0]//sp; cols=G.shape[1]
    G=G.reshape((sp,)+(2,)*nb+(rows>>nb,cols))
    for b in order: G=halve(G,"dp",b,1)
    G=G.reshape((2,)*bits_of(sp)+G.shape[1:])
    for b in range(bits_of(sp)): G=halve(G,"sp",b,bits_of(sp)-1-b)
    for b in reversed(order): G=double(G,b)
    return G.reshape(rows,cols).astype(jnp.float32)
def on_device(inputs,out_grad,segment_ids,positions,norm1_gain,norm1_bias,norm2_gain,norm2_bias,query_weight,query_bias,key_weight,key_bias,value_weight,value_bias,output_weight,output_bias,hidden_weight,hidden_bias,down_weight,down_bias):
    f32=jnp.float32
    sp=lax.axis_size("sp"); dp=lax.axis_size("dp"); s=lax.axis_index("sp")
    R,T,D=inputs.shape; hd=key_weight.shape[1]; rot=key_bias.shape[0]
    N=R*T
    x=inputs.reshape(N,D); g=out_grad.reshape(N,D)
    vec=lambda v: v.astype(f32)[None,:]
    pos=lax.dynamic_slice_in_dim(positions,s*T,T,1)
    pf=pos.astype(f32).reshape(N)
    freq=10000.0**(-(jnp.arange(rot//2,dtype=f32)*2.0)/rot)
    ang=pf[None,:]*freq[:,None]
    ds=(jnp.arange(T,dtype=f32)[None,:]-pos.astype(f32)).reshape(1,N)
    cs=jnp.concatenate([jnp.cos(ang),jnp.sin(ang),ds,jnp.zeros((7,N),f32)],0)
    wkv=jnp.concatenate([key_weight,value_weight],1)
    bkv=jnp.concatenate([key_bias.astype(f32),jnp.zeros((hd-rot,),f32),value_bias.astype(f32)])[None,:]
    g1,b1,g2,b2=map(vec,(norm1_gain,norm1_bias,norm2_gain,norm2_bias))
    q,kv,do,tab=pre(x,g,cs,query_weight,wkv,output_weight,vec(query_bias),bkv,g1,b1)
    kvp=lax.ppermute(kv,"sp",[(i,i+1) for i in range(0,sp,2)])
    br,dm,dw1,dw2,db1=mlp(x,g,hidden_weight,down_weight,vec(hidden_bias),g2,b2,bw=512,rows=512)
    o,dq,dkv=attn(pos[:,0],q,do,kv,kvp,tab,T=T)
    drecv=lax.ppermute(dkv[:,:,:T].astype(jnp.bfloat16),"sp",[(i+1,i) for i in range(0,sp,2)])
    dwq,dwo,qb=wgrad(x,g,o,dq,g1,b1)
    lo,ig,sm,dwkv,kvb=post(x,g,o,dq,br,dm,dkv,drecv,tab,query_weight,wkv,output_weight,vec(output_bias),vec(down_bias),g1,b1,g2,T=T)
    nb=bits_of(dp)
    A=tuple(range(nb)); B=(0,)+tuple(range(nb-1,0,-1))
    rw1=reduce_stream(dw1,A); rw2=reduce_stream(dw2,B)
    rq=reduce_stream(dwq,A); ro=reduce_stream(dwo,B)
    rkv=reduce_stream(dwkv.astype(jnp.bfloat16),A)
    small=jnp.concatenate([sm[0],sm[1],sm[2],sm[3],sm[4],qb[0],db1[0],kvb[0]])
    small=lax.psum(small,("dp","sp"))
    def piece(a,n): return lax.dynamic_slice_in_dim(a,s*(n//sp),n//sp)
    n1g,n1b,n2g,n2b,ob,qbg=[piece(small[i*D:(i+1)*D],D) for i in range(6)]
    F=hidden_weight.shape[1]
    hb=piece(small[6*D:6*D+F],F)
    kb=piece(small[6*D+F:6*D+F+rot],rot)
    vb=piece(small[6*D+F+hd:6*D+F+2*hd],hd)
    return (lo.reshape(R,T,D),ig.reshape(R,T,D),n1g,n1b,n2g,n2b,rq,qbg,rkv[:,:hd],kb,rkv[:,hd:],vb,ro,ob,rw1,hb,rw2,ob)
def solution(mesh):
    t=P("dp","sp",None); m=P("dp",None); w=P()
    v=P("sp"); v2=P("sp",None)
    return jax.shard_map(on_device,mesh=mesh,in_specs=(t,t,m,m)+(w,)*16,
        out_specs=(t,t,v,v,v,v,v2,v,v2,v,v2,v,v2,v,v2,v,v2,v),check_vma=False)
```

time: 1710 us -> 344 us (0.20)
  waiting for transfers between devices: 927 us -> 102 us
  matrix products: 281 us -> 0 us
  local copies, waits for them, and re-layouts: 289 us -> 28.3 us
  Pallas kernels: 0 us -> 98 us
  other arithmetic: 104 us -> 19.7 us
  starting transfers between devices: 35.8 us -> 52.9 us
    unnamed x5 -> x0, waiting for transfers between devices: 789 us -> none
    dot_general x84 -> x0, matrix products: 281 us -> none  [the longest x12 53.4 us: times_transposed(): lax.dot_general(matrix_a, matrix_b, (((1,), (1,)), ((), ())), preferred_e...]
    unnamed x319 -> x72, local copies, waits for them, and re-layouts: 155 us -> 9.61 us
    ppermute x0 -> x42, waiting for transfers between devices: none -> 102 us  [the longest x25 68.9 us: halve(): recv = lax.ppermute(send, axis_name, pair_perm(n, bit))]
    pallas_call x0 -> x5, Pallas kernels: none -> 98 us  [the longest x1 36.6 us: mlp(): pl.pallas_call(functools.partial(mlp_kernel, rows=rows), grid=(n,), in_sp...]
    psum x1 -> x0, waiting for transfers between devices: 86.1 us -> none  [on_device(): summed = lax.psum(own_row, 'dp').reshape(-1)]
    slice x23 -> x8, local copies, waits for them, and re-layouts: 61.8 us -> 3.36 us  [the longest x1 1.77 us: on_device(): dkv[:, :, :T].astype(jnp.bfloat16)]
    ppermute x0 -> x42, starting transfers between devices: none -> 52.9 us  [the longest x25 35.1 us: halve(): recv = lax.ppermute(send, axis_name, pair_perm(n, bit))]
  transfers between devices with their start and end apart: 12 -> 42, of which waited for: 8 -> 30; matrix products, arithmetic and copies ran while one was open for 17% -> 10% of each run, Pallas kernels for 0% -> 27%
where the time goes in v1:
time: 344 us; the launch traced here: 343 us
  waiting for transfers between devices  102 us (30%)
  Pallas kernels  98 us (28%)
  starting transfers between devices  52.9 us (15%)
  blocking collectives  40.8 us (12%)
  local copies, waits for them, and re-layouts  28.3 us (8%)
  other arithmetic  19.7 us (6%)
    ppermute x25, waiting for transfers between devices, halve(): recv = lax.ppermute(send, axis_name, pair_perm(n, bit))  68.9 us
    psum x1, blocking collectives, on_device(): small = lax.psum(small, ('dp', 'sp'))  40.8 us
    pallas_call x1, Pallas kernels, mlp(): pl.pallas_call(functools.partial(mlp_kernel, rows=rows), grid=(n,), in_sp...  36.6 us
    pallas_call x1, Pallas kernels, attn(): pl.pallas_call(functools.partial(attn_kernel, QB=QB), grid_spec=pltpu.Pre...  36.3 us
    ppermute x25, starting transfers between devices, halve(): recv = lax.ppermute(send, axis_name, pair_perm(n, bit))  35.1 us
    ppermute x15, waiting for transfers between devices, double(): recv = lax.ppermute(own, 'dp', pair_perm(n, bit))  20.7 us
    ppermute x1, waiting for transfers between devices, on_device(): lax.ppermute(dkv[:, :, :T].astype(jnp.bfloat16), 'sp', [(i + 1, i) for i...  12.4 us
    pallas_call x1, Pallas kernels, post(): pl.pallas_call(post_kernel, grid=(N // B,), in_specs=[row(D)] * 6 + [pl.B...  12 us
  transfers between devices with their start and end apart: 42, of which 30 were waited for; matrix products, arithmetic and copies ran while one was open for 10% of the time, Pallas kernels for 27%

profile of v1, /device:TPU:0, one launch (start us, length us, event | category | flops | bytes accessed | tf_op | source)
XLA Modules:
  0.0 343.4 jit_solution(8688202728296071992)
XLA Ops:
  9.6 6.6 %pre.1 = (bf16[1024,768]{1,0:T(8,128)(2,1)S(1)}, bf16[1024,128]{1,0:T(8,128)(2,1)S(1)}, bf16[1024,768]{1,0:T(8,128)(2,1)}, f32[1024,256]{1,0:T(8,128)S(1)}) custom-call(bf16[1024,768]{1,0:T(8,128)(2,1)} %bitcast.227, bf16[1024,768]{1,0:T(8,128)(2,1)} %bitcast.231, f32[24,1024]{1,0:T(8,128)S(1)} %maximum_maximum_fusion.cs_ref, ...), custom_call_target="tpu_custom_call" | custom-call | tf_op jit(solution)/shard_map/pre/pallas_call | solution.py:92
  18.3 4.9 %collective-permute-start = (bf16[1024,128]{1,0:T(8,128)(2,1)S(1)}, bf16[1024,128]{1,0:T(8,128)(2,1)S(1)}, u32[]{:S(2)}, u32[]{:S(2)}) collective-permute-start(bf16[1024,128]{1,0:T(8,128)(2,1)S(1)} %get-tuple-element.40.kv_ref), channel_id=1, source_target_pairs={{0,1},{2,3},{4,5},{6,7},{8,9},{10,11},{12,13},{14,15},{16,17},{18,... | collective-permute-start | bytes 786440 | tf_op jit(solution)/shard_map/ppermute | solution.py:257
  25.0 36.6 %mlp.1 = (f32[1024,768]{1,0:T(8,128)}, f32[1024,768]{1,0:T(8,128)}, bf16[768,3072]{1,0:T(8,128)(2,1)}, bf16[3072,768]{1,0:T(8,128)(2,1)}, f32[1,3072]{1,0:T(1,128)}) custom-call(bf16[1024,768]{1,0:T(8,128)(2,1)} %bitcast.228, bf16[1024,768]{1,0:T(8,128)(2,1)} %bitcast.232, bf16[768,3072]{1,0:T(8,128)(2,1)} %w1_ref.1, bf16[3072,768]{1,0:T(8,128)(2,1)} %w2_ref.1, ...), custom_call_target="tpu_custom_call" | custom-call | tf_op jit(solution)/shard_map/mlp/pallas_call | solution.py:50
  61.6 3.2 dynamic-slice_bitcast_fusion
  67.0 36.3 %attn.1 = (bf16[1024,768]{1,0:T(8,128)(2,1)}, bf16[1024,768]{1,0:T(8,128)(2,1)}, f32[2,128,1024]{2,1,0:T(8,128)}) custom-call(s32[2]{0:T(128)} %fusion.31.p0_ref, bf16[1024,768]{1,0:T(8,128)(2,1)} %copy-done.6, bf16[1024,768]{1,0:T(8,128)(2,1)} %get-tuple-element.39.do_ref, bf16[1024,128]{1,0:T(8,128)(2,1)} %copy-done.11, bf16[1024,128]{1,0:T(8,128)(2,1)} %copy-done.15, ...), custom_call_target="tpu_custom_call" | custom-call | tf_op jit(solution)/shard_map/attn/pallas_call | solution.py:153
  109.7 6.5 %wgrad.1 = (bf16[768,768]{1,0:T(8,128)(2,1)S(1)}, bf16[768,768]{1,0:T(8,128)(2,1)S(1)}, f32[1,768]{1,0:T(1,128)S(1)}) custom-call(bf16[1024,768]{1,0:T(8,128)(2,1)S(1)} %bitcast.230, bf16[1024,768]{1,0:T(8,128)(2,1)S(1)} %bitcast.234, bf16[1024,768]{1,0:T(8,128)(2,1)} %get-tuple-element.42.o_ref, bf16[1024,768]{1,0:T(8,128)(2,1)} %get-tuple-element.43.dq_ref, ...), custom_call_target="tpu_custom_call" | custom-call | tf_op jit(solution)/shard_map/wgrad/pallas_call | solution.py:176
  117.7 12.4 %collective-permute-done.1.dr_ref = bf16[2,128,512]{2,1,0:T(8,128)(2,1)} collective-permute-done((bf16[2,128,512]{2,1,0:T(8,128)(2,1)}, bf16[2,128,512]{2,1,0:T(8,128)(2,1)}, u32[]{:S(2)}, u32[]{:S(2)}) %collective-permute-start.1) | collective-permute-done | bytes 262176 | tf_op jit(solution)/shard_map/ppermute | solution.py:260
  130.1 12.0 %post.1 = (bf16[1024,768]{1,0:T(8,128)(2,1)}, f32[1024,768]{1,0:T(8,128)}, f32[8,768]{1,0:T(8,128)}, f32[768,128]{1,0:T(8,128)}, f32[1,128]{1,0:T(1,128)}) custom-call(bf16[1024,768]{1,0:T(8,128)(2,1)} %bitcast.229, bf16[1024,768]{1,0:T(8,128)(2,1)} %bitcast.233, bf16[1024,768]{1,0:T(8,128)(2,1)} %get-tuple-element.42.o_ref, ...), custom_call_target="tpu_custom_call" | custom-call | tf_op jit(solution)/shard_map/post/pallas_call | solution.py:208
  146.2 2.6 collective-permute-done.11
  150.5 2.3 collective-permute-done.12
  152.8 5.1 %collective-permute-start.13 = (bf16[2,24,128]{2,1,0:T(8,128)(2,1)S(1)}, bf16[2,24,128]{2,1,0:T(8,128)(2,1)S(1)}, u32[]{:S(2)}, u32[]{:S(2)}) collective-permute-start(bf16[2,24,128]{2,1,0:T(8,128)(2,1)S(1)} %fusion.25), channel_id=1, source_target_pairs={{0,1},{1,0},{2,3},{3,2},{4,5},{5,4},{6,7},{7,6},{8,9},{9,8},{10,11... | collective-permute-start | bytes 36872 | tf_op jit(solution)/shard_map/ppermute | solution.py:224
  157.9 40.8 %psum.7 = f32[7808]{0:T(1024)S(1)} all-reduce(f32[7808]{0:T(1024)S(1)} %constant_dynamic-update-slice_fusion.2), channel_id=1, replica_groups=mesh['dp'=8,'sp'=4] {'dp','sp'}, use_global_device_ids=true, to_apply=%region_0.1 | all-reduce | flops 7808 | bytes 62464 | tf_op jit(solution)/shard_map/psum | solution.py:269
  204.9 2.3 collective-permute-start.15
  216.6 2.1 collective-permute-start.19
  220.9 5.2 %collective-permute-done.19 = bf16[4,2,24,768]{3,2,1,0:T(8,128)(2,1)S(1)} collective-permute-done((bf16[4,2,24,768]{3,2,1,0:T(8,128)(2,1)S(1)}, bf16[4,2,24,768]{3,2,1,0:T(8,128)(2,1)S(1)}, u32[]{:S(2)}, u32[]{:S(2)}) %collective-permute-start.19) | collective-permute-done | bytes 294944 | tf_op jit(solution)/shard_map/ppermute | solution.py:224
  229.5 2.5 collective-permute-done.20
  232.1 2.1 collective-permute-start.21
  239.4 2.4 collective-permute-start.6
  252.9 2.5 fusion
  256.1 2.6 fusion.1
  261.3 22.6 %collective-permute-done.35 = bf16[4,2,96,768]{3,2,1,0:T(8,128)(2,1)S(1)} collective-permute-done((bf16[4,2,96,768]{3,2,1,0:T(8,128)(2,1)S(1)}, bf16[4,2,96,768]{3,2,1,0:T(8,128)(2,1)S(1)}, u32[]{:S(2)}, u32[]{:S(2)}) %collective-permute-start.35) | collective-permute-done | bytes 1179680 | tf_op jit(solution)/shard_map/ppermute | solution.py:224
  284.8 2.3 collective-permute-done.27
  287.6 2.1 collective-permute-start.28
  290.6 9.0 %collective-permute-done.36 = bf16[4,96,768]{2,1,0:T(8,128)(2,1)S(1)} collective-permute-done((bf16[4,96,768]{2,1,0:T(8,128)(2,1)S(1)}, bf16[4,96,768]{2,1,0:T(8,128)(2,1)S(1)}, u32[]{:S(2)}, u32[]{:S(2)}) %collective-permute-start.36) | collective-permute-done | bytes 589856 | tf_op jit(solution)/shard_map/ppermute | solution.py:224
  302.2 2.4 collective-permute-start.29
  304.6 5.1 %collective-permute-done.37 = bf16[2,96,768]{2,1,0:T(8,128)(2,1)S(1)} collective-permute-done((bf16[2,96,768]{2,1,0:T(8,128)(2,1)S(1)}, bf16[2,96,768]{2,1,0:T(8,128)(2,1)S(1)}, u32[]{:S(2)}, u32[]{:S(2)}) %collective-permute-start.37) | collective-permute-done | bytes 294944 | tf_op jit(solution)/shard_map/ppermute | solution.py:224
  309.9 2.4 collective-permute-start.38
  312.2 5.3 %collective-permute-done.29 = bf16[2,24,3072]{2,1,0:T(8,128)(2,1)S(1)} collective-permute-done((bf16[2,24,3072]{2,1,0:T(8,128)(2,1)S(1)}, bf16[2,24,3072]{2,1,0:T(8,128)(2,1)S(1)}, u32[]{:S(2)}, u32[]{:S(2)}) %collective-permute-start.29) | collective-permute-done | bytes 294944 | tf_op jit(solution)/shard_map/ppermute | solution.py:224
  319.8 5.5 %collective-permute-done.30 = bf16[24,3072]{1,0:T(8,128)(2,1)S(1)} collective-permute-done((bf16[24,3072]{1,0:T(8,128)(2,1)S(1)}, bf16[24,3072]{1,0:T(8,128)(2,1)S(1)}, u32[]{:S(2)}, u32[]{:S(2)}) %collective-permute-start.30) | collective-permute-done | bytes 147488 | tf_op jit(solution)/shard_map/ppermute | solution.py:224
  327.6 4.5 %collective-permute-done.31 = bf16[24,3072]{1,0:T(8,128)(2,1)S(1)} collective-permute-done((bf16[24,3072]{1,0:T(8,128)(2,1)S(1)}, bf16[24,3072]{1,0:T(8,128)(2,1)S(1)}, u32[]{:S(2)}, u32[]{:S(2)}) %collective-permute-start.31) | collective-permute-done | bytes 147488 | tf_op jit(solution)/shard_map/ppermute | solution.py:229
  333.9 2.5 collective-permute-done.40
  336.6 2.3 collective-permute-done.32
  (259 shorter events, 84.7 us)
Async XLA Ops:
  18.3 48.0 %collective-permute-start = (bf16[1024,128]{1,0:T(8,128)(2,1)S(1)}, bf16[1024,128]{1,0:T(8,128)(2,1)S(1)}, u32[]{:S(2)}, u32[]{:S(2)}) collective-permute-start(bf16[1024,128]{1,0:T(8,128)(2,1)S(1)} %get-tuple-element.40.kv_ref), channel_id=1, source_target_pairs={{0,1},{2,3},{4,5},{6,7},{8,9},{10,11},{12,13},{14,15},{16,17},{18,... | collective-permute-start | bytes 786440 | tf_op jit(solution)/shard_map/ppermute | solution.py:257
  64.9 188.0 %collective-permute-start.34 = (bf16[4,2,2,96,768]{4,3,2,1,0:T(8,128)(2,1)}, bf16[4,2,2,96,768]{4,3,2,1,0:T(8,128)(2,1)}, u32[]{:S(2)}, u32[]{:S(2)}) collective-permute-start(bf16[4,2,2,96,768]{4,3,2,1,0:T(8,128)(2,1)} %dynamic-slice_bitcast_fusion), channel_id=1, source_target_pairs={{0,4},{4,0},{8,12},{12,8},{16,20},{20,16},{24,28},{28,24},{1,5},{5... | collective-permute-start | bytes 7077896 | tf_op jit(solution)/shard_map/ppermute | solution.py:224
  105.0 25.1 %collective-permute-start.1 = (bf16[2,128,512]{2,1,0:T(8,128)(2,1)}, bf16[2,128,512]{2,1,0:T(8,128)(2,1)}, u32[]{:S(2)}, u32[]{:S(2)}) collective-permute-start(bf16[2,128,512]{2,1,0:T(8,128)(2,1)} %slice.91), channel_id=1, source_target_pairs={{1,0},{3,2},{5,4},{7,6},{9,8},{11,10},{13,12},{15,14},{17,16},{19,... | collective-permute-start | bytes 786440 | tf_op jit(solution)/shard_map/ppermute | solution.py:260
  108.0 148.1 %collective-permute-start.26 = (bf16[4,2,2,24,3072]{4,3,2,1,0:T(8,128)(2,1)}, bf16[4,2,2,24,3072]{4,3,2,1,0:T(8,128)(2,1)}, u32[]{:S(2)}, u32[]{:S(2)}) collective-permute-start(bf16[4,2,2,24,3072]{4,3,2,1,0:T(8,128)(2,1)} %dynamic-slice_bitcast_fusion.1), channel_id=1, source_target_pairs={{0,4},{4,0},{8,12},{12,8},{16,20},{20,16},{24,28},{28,24},{1,5},{5... | collective-permute-start | bytes 7077896 | tf_op jit(solution)/shard_map/ppermute | solution.py:224
  116.3 99.0 %collective-permute-start.18 = (bf16[4,2,2,24,768]{4,3,2,1,0:T(8,128)(2,1)S(1)}, bf16[4,2,2,24,768]{4,3,2,1,0:T(8,128)(2,1)}, u32[]{:S(2)}, u32[]{:S(2)}) collective-permute-start(bf16[4,2,2,24,768]{4,3,2,1,0:T(8,128)(2,1)S(1)} %dynamic-slice_bitcast_fusion.6), channel_id=1, source_target_pairs={{0,4},{4,0},{8,12},{12,8},{16,20},{20,16},{24,28},{28,24},{1,5},{5... | collective-permute-start | bytes 1769480 | tf_op jit(solution)/shard_map/ppermute | solution.py:224
  117.7 101.1 %collective-permute-start.2 = (bf16[4,2,2,24,768]{4,3,2,1,0:T(8,128)(2,1)S(1)}, bf16[4,2,2,24,768]{4,3,2,1,0:T(8,128)(2,1)}, u32[]{:S(2)}, u32[]{:S(2)}) collective-permute-start(bf16[4,2,2,24,768]{4,3,2,1,0:T(8,128)(2,1)S(1)} %dynamic-slice_bitcast_fusion.7), channel_id=1, source_target_pairs={{0,4},{4,0},{8,12},{12,8},{16,20},{20,16},{24,28},{28,24},{1,5},{5... | collective-permute-start | bytes 1769480 | tf_op jit(solution)/shard_map/ppermute | solution.py:224
  152.8 45.9 %collective-permute-start.13 = (bf16[2,24,128]{2,1,0:T(8,128)(2,1)S(1)}, bf16[2,24,128]{2,1,0:T(8,128)(2,1)S(1)}, u32[]{:S(2)}, u32[]{:S(2)}) collective-permute-start(bf16[2,24,128]{2,1,0:T(8,128)(2,1)S(1)} %fusion.25), channel_id=1, source_target_pairs={{0,1},{1,0},{2,3},{3,2},{4,5},{5,4},{6,7},{7,6},{8,9},{9,8},{10,11... | collective-permute-start | bytes 36872 | tf_op jit(solution)/shard_map/ppermute | solution.py:224
  198.8 6.1 %collective-permute-start.14 = (bf16[24,128]{1,0:T(8,128)(2,1)S(1)}, bf16[24,128]{1,0:T(8,128)(2,1)S(1)}, u32[]{:S(2)}, u32[]{:S(2)}) collective-permute-start(bf16[24,128]{1,0:T(8,128)(2,1)S(1)} %fusion.28), channel_id=1, source_target_pairs={{0,2},{1,3},{2,0},{3,1},{4,6},{5,7},{6,4},{7,5},{8,10},{9,11},{10,... | collective-permute-start | bytes 18440 | tf_op jit(solution)/shard_map/ppermute | solution.py:224
  216.6 9.4 %collective-permute-start.19 = (bf16[4,2,24,768]{3,2,1,0:T(8,128)(2,1)S(1)}, bf16[4,2,24,768]{3,2,1,0:T(8,128)(2,1)S(1)}, u32[]{:S(2)}, u32[]{:S(2)}) collective-permute-start(bf16[4,2,24,768]{3,2,1,0:T(8,128)(2,1)S(1)} %dynamic-slice_bitcast_fusion.10), channel_id=1, source_target_pairs={{0,16},{4,20},{8,24},{12,28},{16,0},{20,4},{24,8},{28,12},{1,17},{... | collective-permute-start | bytes 884744 | tf_op jit(solution)/shard_map/ppermute | solution.py:224
  220.0 9.1 %collective-permute-start.3 = (bf16[4,2,24,768]{3,2,1,0:T(8,128)(2,1)S(1)}, bf16[4,2,24,768]{3,2,1,0:T(8,128)(2,1)S(1)}, u32[]{:S(2)}, u32[]{:S(2)}) collective-permute-start(bf16[4,2,24,768]{3,2,1,0:T(8,128)(2,1)S(1)} %dynamic-slice_bitcast_fusion.11), channel_id=1, source_target_pairs={{0,8},{4,12},{8,0},{12,4},{16,24},{20,28},{24,16},{28,20},{1,9},{5... | collective-permute-start | bytes 884744 | tf_op jit(solution)/shard_map/ppermute | solution.py:224
  226.2 5.8 %collective-permute-start.20 = (bf16[4,24,768]{2,1,0:T(8,128)(2,1)S(1)}, bf16[4,24,768]{2,1,0:T(8,128)(2,1)S(1)}, u32[]{:S(2)}, u32[]{:S(2)}) collective-permute-start(bf16[4,24,768]{2,1,0:T(8,128)(2,1)S(1)} %dynamic-slice_bitcast_fusion.14), channel_id=1, source_target_pairs={{0,8},{4,12},{8,0},{12,4},{16,24},{20,28},{24,16},{28,20},{1,9},{5... | collective-permute-start | bytes 442376 | tf_op jit(solution)/shard_map/ppermute | solution.py:224
  229.2 5.2 %collective-permute-start.4 = (bf16[4,24,768]{2,1,0:T(8,128)(2,1)S(1)}, bf16[4,24,768]{2,1,0:T(8,128)(2,1)S(1)}, u32[]{:S(2)}, u32[]{:S(2)}) collective-permute-start(bf16[4,24,768]{2,1,0:T(8,128)(2,1)S(1)} %dynamic-slice_bitcast_fusion.15), channel_id=1, source_target_pairs={{0,16},{4,20},{8,24},{12,28},{16,0},{20,4},{24,8},{28,12},{1,17},{... | collective-permute-start | bytes 442376 | tf_op jit(solution)/shard_map/ppermute | solution.py:224
  232.1 5.2 %collective-permute-start.21 = (bf16[2,24,768]{2,1,0:T(8,128)(2,1)S(1)}, bf16[2,24,768]{2,1,0:T(8,128)(2,1)S(1)}, u32[]{:S(2)}, u32[]{:S(2)}) collective-permute-start(bf16[2,24,768]{2,1,0:T(8,128)(2,1)S(1)} %dynamic-slice_bitcast_fusion.16), channel_id=1, source_target_pairs={{0,1},{1,0},{2,3},{3,2},{4,5},{5,4},{6,7},{7,6},{8,9},{9,8},{10,11... | collective-permute-start | bytes 221192 | tf_op jit(solution)/shard_map/ppermute | solution.py:224
  234.5 4.8 %collective-permute-start.5 = (bf16[2,24,768]{2,1,0:T(8,128)(2,1)S(1)}, bf16[2,24,768]{2,1,0:T(8,128)(2,1)S(1)}, u32[]{:S(2)}, u32[]{:S(2)}) collective-permute-start(bf16[2,24,768]{2,1,0:T(8,128)(2,1)S(1)} %dynamic-slice_bitcast_fusion.17), channel_id=1, source_target_pairs={{0,1},{1,0},{2,3},{3,2},{4,5},{5,4},{6,7},{7,6},{8,9},{9,8},{10,11... | collective-permute-start | bytes 221192 | tf_op jit(solution)/shard_map/ppermute | solution.py:224
  237.3 4.9 %collective-permute-start.22 = (bf16[24,768]{1,0:T(8,128)(2,1)S(1)}, bf16[24,768]{1,0:T(8,128)(2,1)S(1)}, u32[]{:S(2)}, u32[]{:S(2)}) collective-permute-start(bf16[24,768]{1,0:T(8,128)(2,1)S(1)} %dynamic-slice_bitcast_fusion.19), channel_id=1, source_target_pairs={{0,2},{1,3},{2,0},{3,1},{4,6},{5,7},{6,4},{7,5},{8,10},{9,11},{10,... | collective-permute-start | bytes 110600 | tf_op jit(solution)/shard_map/ppermute | solution.py:224
  239.4 4.9 %collective-permute-start.6 = (bf16[24,768]{1,0:T(8,128)(2,1)S(1)}, bf16[24,768]{1,0:T(8,128)(2,1)S(1)}, u32[]{:S(2)}, u32[]{:S(2)}) collective-permute-start(bf16[24,768]{1,0:T(8,128)(2,1)S(1)} %dynamic-slice_bitcast_fusion.20), channel_id=1, source_target_pairs={{0,2},{1,3},{2,0},{3,1},{4,6},{5,7},{6,4},{7,5},{8,10},{9,11},{10,... | collective-permute-start | bytes 110600 | tf_op jit(solution)/shard_map/ppermute | solution.py:224
  246.3 4.4 %collective-permute-start.24 = (bf16[2,24,768]{2,1,0:T(8,128)(2,1)S(1)}, bf16[2,24,768]{2,1,0:T(8,128)(2,1)S(1)}, u32[]{:S(2)}, u32[]{:S(2)}) collective-permute-start(bf16[2,24,768]{2,1,0:T(8,128)(2,1)S(1)} %bitcast_dynamic-update-slice_fusion.10), channel_id=1, source_target_pairs={{0,16},{4,20},{8,24},{12,28},{16,0},{20,4},{24,8},{28,12},{1,17},{... | collective-permute-start | bytes 221192 | tf_op jit(solution)/shard_map/ppermute | solution.py:229
  248.3 4.4 %collective-permute-start.8 = (bf16[2,24,768]{2,1,0:T(8,128)(2,1)S(1)}, bf16[2,24,768]{2,1,0:T(8,128)(2,1)S(1)}, u32[]{:S(2)}, u32[]{:S(2)}) collective-permute-start(bf16[2,24,768]{2,1,0:T(8,128)(2,1)S(1)} %bitcast_dynamic-update-slice_fusion.11), channel_id=1, source_target_pairs={{0,8},{4,12},{8,0},{12,4},{16,24},{20,28},{24,16},{28,20},{1,9},{5... | collective-permute-start | bytes 221192 | tf_op jit(solution)/shard_map/ppermute | solution.py:229
  250.6 9.7 %collective-permute-start.25 = (bf16[2,2,24,768]{3,2,1,0:T(8,128)(2,1)S(1)}, bf16[2,2,24,768]{3,2,1,0:T(8,128)(2,1)S(1)}, u32[]{:S(2)}, u32[]{:S(2)}) collective-permute-start(bf16[2,2,24,768]{3,2,1,0:T(8,128)(2,1)S(1)} %bitcast_dynamic-update-slice_fusion.8), channel_id=1, source_target_pairs={{0,4},{4,0},{8,12},{12,8},{16,20},{20,16},{24,28},{28,24},{1,5},{5... | collective-permute-start | bytes 442376 | tf_op jit(solution)/shard_map/ppermute | solution.py:229
  252.7 7.7 %collective-permute-start.9 = (bf16[2,2,24,768]{3,2,1,0:T(8,128)(2,1)S(1)}, bf16[2,2,24,768]{3,2,1,0:T(8,128)(2,1)S(1)}, u32[]{:S(2)}, u32[]{:S(2)}) collective-permute-start(bf16[2,2,24,768]{3,2,1,0:T(8,128)(2,1)S(1)} %bitcast_dynamic-update-slice_fusion.9), channel_id=1, source_target_pairs={{0,4},{4,0},{8,12},{12,8},{16,20},{20,16},{24,28},{28,24},{1,5},{5... | collective-permute-start | bytes 442376 | tf_op jit(solution)/shard_map/ppermute | solution.py:229
  255.5 28.4 %collective-permute-start.35 = (bf16[4,2,96,768]{3,2,1,0:T(8,128)(2,1)S(1)}, bf16[4,2,96,768]{3,2,1,0:T(8,128)(2,1)S(1)}, u32[]{:S(2)}, u32[]{:S(2)}) collective-permute-start(bf16[4,2,96,768]{3,2,1,0:T(8,128)(2,1)S(1)} %dynamic-slice_bitcast_fusion.2), channel_id=1, source_target_pairs={{0,16},{4,20},{8,24},{12,28},{16,0},{20,4},{24,8},{28,12},{1,17},{... | collective-permute-start | bytes 3538952 | tf_op jit(solution)/shard_map/ppermute | solution.py:224
  258.7 28.4 %collective-permute-start.27 = (bf16[4,2,24,3072]{3,2,1,0:T(8,128)(2,1)S(1)}, bf16[4,2,24,3072]{3,2,1,0:T(8,128)(2,1)S(1)}, u32[]{:S(2)}, u32[]{:S(2)}) collective-permute-start(bf16[4,2,24,3072]{3,2,1,0:T(8,128)(2,1)S(1)} %dynamic-slice_bitcast_fusion.3), channel_id=1, source_target_pairs={{0,8},{4,12},{8,0},{12,4},{16,24},{20,28},{24,16},{28,20},{1,9},{5... | collective-permute-start | bytes 3538952 | tf_op jit(solution)/shard_map/ppermute | solution.py:224
  284.2 15.3 %collective-permute-start.36 = (bf16[4,96,768]{2,1,0:T(8,128)(2,1)S(1)}, bf16[4,96,768]{2,1,0:T(8,128)(2,1)S(1)}, u32[]{:S(2)}, u32[]{:S(2)}) collective-permute-start(bf16[4,96,768]{2,1,0:T(8,128)(2,1)S(1)} %dynamic-slice_bitcast_fusion.4), channel_id=1, source_target_pairs={{0,8},{4,12},{8,0},{12,4},{16,24},{20,28},{24,16},{28,20},{1,9},{5... | collective-permute-start | bytes 1769480 | tf_op jit(solution)/shard_map/ppermute | solution.py:224
  287.6 14.5 %collective-permute-start.28 = (bf16[4,24,3072]{2,1,0:T(8,128)(2,1)S(1)}, bf16[4,24,3072]{2,1,0:T(8,128)(2,1)S(1)}, u32[]{:S(2)}, u32[]{:S(2)}) collective-permute-start(bf16[4,24,3072]{2,1,0:T(8,128)(2,1)S(1)} %dynamic-slice_bitcast_fusion.5), channel_id=1, source_target_pairs={{0,16},{4,20},{8,24},{12,28},{16,0},{20,4},{24,8},{28,12},{1,17},{... | collective-permute-start | bytes 1769480 | tf_op jit(solution)/shard_map/ppermute | solution.py:224
  299.7 10.0 %collective-permute-start.37 = (bf16[2,96,768]{2,1,0:T(8,128)(2,1)S(1)}, bf16[2,96,768]{2,1,0:T(8,128)(2,1)S(1)}, u32[]{:S(2)}, u32[]{:S(2)}) collective-permute-start(bf16[2,96,768]{2,1,0:T(8,128)(2,1)S(1)} %dynamic-slice_bitcast_fusion.8), channel_id=1, source_target_pairs={{0,1},{1,0},{2,3},{3,2},{4,5},{5,4},{6,7},{7,6},{8,9},{9,8},{10,11... | collective-permute-start | bytes 884744 | tf_op jit(solution)/shard_map/ppermute | solution.py:224
  302.2 15.3 %collective-permute-start.29 = (bf16[2,24,3072]{2,1,0:T(8,128)(2,1)S(1)}, bf16[2,24,3072]{2,1,0:T(8,128)(2,1)S(1)}, u32[]{:S(2)}, u32[]{:S(2)}) collective-permute-start(bf16[2,24,3072]{2,1,0:T(8,128)(2,1)S(1)} %dynamic-slice_bitcast_fusion.9), channel_id=1, source_target_pairs={{0,1},{1,0},{2,3},{3,2},{4,5},{5,4},{6,7},{7,6},{8,9},{9,8},{10,11... | collective-permute-start | bytes 884744 | tf_op jit(solution)/shard_map/ppermute | solution.py:224
  309.9 8.7 %collective-permute-start.38 = (bf16[96,768]{1,0:T(8,128)(2,1)S(1)}, bf16[96,768]{1,0:T(8,128)(2,1)S(1)}, u32[]{:S(2)}, u32[]{:S(2)}) collective-permute-start(bf16[96,768]{1,0:T(8,128)(2,1)S(1)} %dynamic-slice_bitcast_fusion.12), channel_id=1, source_target_pairs={{0,2},{1,3},{2,0},{3,1},{4,6},{5,7},{6,4},{7,5},{8,10},{9,11},{10,... | collective-permute-start | bytes 442376 | tf_op jit(solution)/shard_map/ppermute | solution.py:224
  317.6 7.7 %collective-permute-start.30 = (bf16[24,3072]{1,0:T(8,128)(2,1)S(1)}, bf16[24,3072]{1,0:T(8,128)(2,1)S(1)}, u32[]{:S(2)}, u32[]{:S(2)}) collective-permute-start(bf16[24,3072]{1,0:T(8,128)(2,1)S(1)} %dynamic-slice_bitcast_fusion.13), channel_id=1, source_target_pairs={{0,2},{1,3},{2,0},{3,1},{4,6},{5,7},{6,4},{7,5},{8,10},{9,11},{10,... | collective-permute-start | bytes 442376 | tf_op jit(solution)/shard_map/ppermute | solution.py:224
  318.5 8.8 %collective-permute-start.39 = (bf16[96,768]{1,0:T(8,128)(2,1)S(1)}, bf16[96,768]{1,0:T(8,128)(2,1)S(1)}, u32[]{:S(2)}, u32[]{:S(2)}) collective-permute-start(bf16[96,768]{1,0:T(8,128)(2,1)S(1)} %fusion.12), channel_id=1, source_target_pairs={{0,8},{4,12},{8,0},{12,4},{16,24},{20,28},{24,16},{28,20},{1,9},{5... | collective-permute-start | bytes 442376 | tf_op jit(solution)/shard_map/ppermute | solution.py:229
  325.4 6.7 %collective-permute-start.31 = (bf16[24,3072]{1,0:T(8,128)(2,1)S(1)}, bf16[24,3072]{1,0:T(8,128)(2,1)S(1)}, u32[]{:S(2)}, u32[]{:S(2)}) collective-permute-start(bf16[24,3072]{1,0:T(8,128)(2,1)S(1)} %fusion.13), channel_id=1, source_target_pairs={{0,16},{4,20},{8,24},{12,28},{16,0},{20,4},{24,8},{28,12},{1,17},{... | collective-permute-start | bytes 442376 | tf_op jit(solution)/shard_map/ppermute | solution.py:229
  327.4 9.1 %collective-permute-start.40 = (bf16[2,96,768]{2,1,0:T(8,128)(2,1)S(1)}, bf16[2,96,768]{2,1,0:T(8,128)(2,1)S(1)}, u32[]{:S(2)}, u32[]{:S(2)}) collective-permute-start(bf16[2,96,768]{2,1,0:T(8,128)(2,1)S(1)} %bitcast_dynamic-update-slice_fusion.4), channel_id=1, source_target_pairs={{0,16},{4,20},{8,24},{12,28},{16,0},{20,4},{24,8},{28,12},{1,17},{... | collective-permute-start | bytes 884744 | tf_op jit(solution)/shard_map/ppermute | solution.py:229
  332.1 6.8 %collective-permute-start.32 = (bf16[2,24,3072]{2,1,0:T(8,128)(2,1)S(1)}, bf16[2,24,3072]{2,1,0:T(8,128)(2,1)S(1)}, u32[]{:S(2)}, u32[]{:S(2)}) collective-permute-start(bf16[2,24,3072]{2,1,0:T(8,128)(2,1)S(1)} %bitcast_dynamic-update-slice_fusion.5), channel_id=1, source_target_pairs={{0,8},{4,12},{8,0},{12,4},{16,24},{20,28},{24,16},{28,20},{1,9},{5... | collective-permute-start | bytes 884744 | tf_op jit(solution)/shard_map/ppermute | solution.py:229
  (39 other events, 800.8 us)
